TPU v7x, 128 devices: a whole 4x4x4 slice. The times are simulated.
128 devices in a mesh: shot: 4 (over z_hi, core), gx: 16 (over x, y), gy: 2 (over z_lo).
Axes of the slice: x: 4, y: 4, z: 4 (z_hi: 2, z_lo: 2; z = z_hi * 2 + z_lo), core: 2. Of those that a mesh axis runs over, the one named last changes fastest.
Arguments:
- wave_now: float32 [4, 4, 512, 64, 128], P('shot', None, 'gx', 'gy'), may hold values from -6 to 6
- wave_prev: float32 [4, 4, 512, 64, 128], P('shot', None, 'gx', 'gy'), may hold values from -6 to 6
- vel_coef: float32 [512, 64, 128], P('gx', 'gy'), may hold values from 0.08 to 0.18
- epsilon: float32 [512, 64, 128], P('gx', 'gy'), may hold values from 0.15 to 0.35
- delta: float32 [512, 64, 128], P('gx', 'gy'), may hold values from 0 to 0.15
- tilt: int32 [512, 64, 128], P('gx', 'gy'), may hold values from 0 to 60
- azimuth: int32 [512, 64, 128], P('gx', 'gy'), may hold values from 0 to 359
- aperture: int32 [4, 16, 2], P('shot', 'gx', 'gy'), may hold values 0 or 1
Outputs:
- wave_final: float32 [4, 4, 512, 64, 128], P('shot', None, 'gx', 'gy')
- image: float32 [512, 64, 128], P('gx', 'gy')
All inputs are finite; a program needn't handle non-finite values. No bound on the sum of `aperture` on one device may be relied on, other than what follows from the above.
Results may differ from a plain program's by a relative error of at most 0.00002.
Values sent between devices are 32-bit elements; how exact they have to be, the bound alone decides.
A program may use at most 128 MiB of HBM per device.

v0:
```python
import math
import jax
import jax.numpy as jnp
from jax import lax
from jax.sharding import PartitionSpec as P

ITERS = 4


def extended(block, sides, width):
    for axis, dim in sides:
        count = lax.axis_size(axis)
        forward = [(i, i + 1) for i in range(count - 1)]
        backward = [(target, source) for source, target in forward]
        low = lax.ppermute(
            lax.slice_in_dim(block, block.shape[dim] - width, None, axis=dim), axis, forward
        )
        high = lax.ppermute(lax.slice_in_dim(block, 0, width, axis=dim), axis, backward)
        block = jnp.concatenate([low, block, high], axis=dim)
    return block


def model_terms(vel_coef, epsilon, delta, tilt, azimuth):
    theta = tilt.astype(jnp.float32) * (math.pi / 180.0)
    phi = azimuth.astype(jnp.float32) * (math.pi / 180.0)
    normal_x = jnp.sin(theta) * jnp.cos(phi)
    normal_y = jnp.sin(theta) * jnp.sin(phi)
    normal_z = jnp.cos(theta)
    gain = 1.0 + 2.0 * epsilon
    root = jnp.sqrt(1.0 + 2.0 * delta)
    return jnp.stack([normal_x, normal_y, normal_z, vel_coef, gain, root], axis=0)


def advance(padded, previous, coef):
    width_x = padded.shape[-3] - 2
    width_y = padded.shape[-2] - 2
    width_z = padded.shape[-1] - 2

    def shifted(off_x, off_y, off_z):
        return padded[
            ...,
            1 + off_x : 1 + off_x + width_x,
            1 + off_y : 1 + off_y + width_y,
            1 + off_z : 1 + off_z + width_z,
        ]

    centre = shifted(0, 0, 0)
    second_x = shifted(1, 0, 0) + shifted(-1, 0, 0) - 2.0 * centre
    second_y = shifted(0, 1, 0) + shifted(0, -1, 0) - 2.0 * centre
    second_z = shifted(0, 0, 1) + shifted(0, 0, -1) - 2.0 * centre
    mixed_xy = 0.25 * (
        shifted(1, 1, 0) - shifted(1, -1, 0) - shifted(-1, 1, 0) + shifted(-1, -1, 0)
    )
    mixed_xz = 0.25 * (
        shifted(1, 0, 1) - shifted(1, 0, -1) - shifted(-1, 0, 1) + shifted(-1, 0, -1)
    )
    mixed_yz = 0.25 * (
        shifted(0, 1, 1) - shifted(0, 1, -1) - shifted(0, -1, 1) + shifted(0, -1, -1)
    )
    normal_x, normal_y, normal_z = (coef[0], coef[1], coef[2])
    speed, gain, root = (coef[3], coef[4], coef[5])
    along = (
        normal_x * normal_x * second_x
        + normal_y * normal_y * second_y
        + normal_z * normal_z * second_z
        + 2.0
        * (
            normal_x * normal_y * mixed_xy
            + normal_x * normal_z * mixed_xz
            + normal_y * normal_z * mixed_yz
        )
    )
    across = second_x + second_y + second_z - along
    pressure = centre[:, 0::2]
    auxiliary = centre[:, 1::2]
    rhs_p = gain * across[:, 0::2] + root * along[:, 1::2]
    rhs_q = root * across[:, 0::2] + along[:, 1::2]
    next_p = 2.0 * pressure - previous[:, 0::2] + speed * rhs_p
    next_q = 2.0 * auxiliary - previous[:, 1::2] + speed * rhs_q
    return jnp.stack([next_p, next_q], axis=2).reshape(centre.shape)


def depth_pad(array):
    return jnp.pad(array, ((0, 0), (0, 0), (0, 0), (0, 0), (1, 1)))


def local(wave_now, wave_prev, vel_coef, epsilon, delta, tilt, azimuth, aperture):
    coef = model_terms(vel_coef, epsilon, delta, tilt, azimuth)
    correlation = jnp.zeros(vel_coef.shape, jnp.float32)
    current, previous = (wave_now, wave_prev)
    for step in range(ITERS):
        widened_now = extended(current, (("gx", 2), ("gy", 3)), 1)
        fresh = advance(depth_pad(widened_now), previous, coef)
        correlation = correlation + fresh[0, 0] * fresh[0, 2]
        previous, current = (current, fresh)
    covered = aperture[0, 0, 0].astype(jnp.float32)
    image = lax.psum(covered * correlation, "shot") / ITERS
    return (current, image)


def solution(mesh):
    return jax.shard_map(
        local,
        mesh=mesh,
        in_specs=(
            P("shot", None, "gx", "gy", None),
            P("shot", None, "gx", "gy", None),
            P("gx", "gy", None),
            P("gx", "gy", None),
            P("gx", "gy", None),
            P("gx", "gy", None),
            P("gx", "gy", None),
            P("shot", "gx", "gy"),
        ),
        out_specs=(P("shot", None, "gx", "gy", None), P("gx", "gy", None)),
        check_vma=False,
    )
```

profile of v0, /device:TPU:1, one launch (start us, length us, event | category | flops | bytes accessed | tf_op | source)
XLA Modules:
  0.0 222.5 jit_solution(3460875306081777361)
XLA Ops:
  8.1 4.0 %collective-permute-start.1 = (f32[1,4,1,32,128]{4,3,2,1,0:T(8,128)S(1)}, f32[1,4,1,32,128]{4,3,2,1,0:T(8,128)S(1)}, u32[]{:S(2)}, u32[]{:S(2)}) collective-permute-start(f32[1,4,1,32,128]{4,3,2,1,0:T(8,128)S(1)} %get-tuple-element.39), channel_id=1, source_target_pairs={{0,2},{2,4},{4,6},{6,8},{8,10},{10,12},{12,14},{14,16},{16,18},{18... | collective-permute-start | bytes 196616 | tf_op jit(solution)/shard_map/ppermute | solution.py:15
  12.2 1.4 collective-permute-start
  13.6 6.1 %fusion.61 = (f32[32,32,128]{2,1,0:T(8,128)S(1)}, f32[32,32,128]{2,1,0:T(8,128)S(1)}, f32[32,32,128]{2,1,0:T(8,128)S(1)}, f32[32,32,128]{2,1,0:T(8,128)S(1)}, f3...) fusion(s32[32,32,128]{2,1,0:T(8,128)} %param.14, s32[32,32,128]{2,1,0:T(8,128)} %param.13), kind=kLoop, calls=%fused_computation.183 | loop fusion | flops 1966080 | bytes 4194304 | tf_op jit(solution)/shard_map/mul | solution.py:63
  20.1 1.4 collective-permute-start.2
  21.6 4.0 %collective-permute-start.3 = (f32[1,4,34,1,128]{4,3,2,1,0:T(1,128)S(1)}, f32[1,4,34,1,128]{4,3,2,1,0:T(1,128)S(1)}, u32[]{:S(2)}, u32[]{:S(2)}) collective-permute-start(f32[1,4,34,1,128]{4,3,2,1,0:T(1,128)S(1)} %get-tuple-element.30), channel_id=1, source_target_pairs={{0,1},{2,3},{4,5},{6,7},{8,9},{10,11},{12,13},{14,15},{16,17},{18,... | collective-permute-start | bytes 208904 | tf_op jit(solution)/shard_map/ppermute | solution.py:15
  26.9 2.7 %select_maximum_fusion.12 = f32[1,4,34,34,130]{4,3,2,1,0:T(8,128)S(1)} fusion(f32[1,4,34,1,128]{4,3,2,1,0:T(1,128)S(1)} %collective-permute-done.2, f32[1,4,34,32,128]{4,3,2,1,0:T(8,128)S(1)} %constant_dynamic-update-slice_fusion, f32[1,4,34,1,128]{4,3,2,1,0:T(1,128)S(1)} %collective-permute-done.3), kind=kLoop, calls=%fused_computation.14 | loop fusion | flops 4808960 | bytes 4771968 | tf_op jit(solution)/shard_map/concatenate | solution.py:19
  29.7 8.4 %add_subtract_fusion.3 = (f32[1,4,32,32,128]{4,3,2,1,0:T(8,128)S(1)}, f32[1,4,32,32,128]{4,3,2,1,0:T(8,128)S(1)}) fusion(f32[1,4,32,32,128]{4,3,2,1,0:T(8,128)S(1)} %copy-done.2, f32[1,4,1,32,128]{4,3,2,1,0:T(8,128)S(1)} %collective-permute-done.1, f32[1,4,1,32,128]{4,3,2,1,0:T(8,128)S(1)} %collective-permute-done, ...), kind=kLoop, calls=%fused_computation.140 | loop fusion | flops 22544384 | bytes 32907264 | tf_op jit(solution)/shard_map/sub | solution.py:73
  38.2 2.5 %add_bitcast_fusion.7 = (f32[1,2,1,32,32,128]{5,4,3,1,2,0:T(8,128)S(1)}, f32[1,2,1,32,32,128]{5,4,3,1,2,0:T(8,128)S(1)}) fusion(f32[1,4,32,32,128]{4,3,2,1,0:T(8,128)} %param.9, f32[1,4,32,32,128]{4,3,2,1,0:T(8,128)S(1)} %get-tuple-element.9, f32[1,4,32,32,128]{4,3,2,1,0:T(8,128)S(1)} %get-tuple-element.8, f32[1,4,32,32,128]{4,3,2,1,0:T(8,128)S(1)} %copy-done.2, ...), kind=kLoop, calls=%fused_computation.148 | loop fusion | flops 3407872 | bytes 9961472 | tf_op jit(solution)/shard_map/stack | solution.py:80
  42.5 4.6 %collective-permute-start.5 = (f32[1,4,1,32,128]{4,3,2,1,0:T(8,128)S(1)}, f32[1,4,1,32,128]{4,3,2,1,0:T(8,128)S(1)}, u32[]{:S(2)}, u32[]{:S(2)}) collective-permute-start(f32[1,4,1,32,128]{4,3,2,1,0:T(8,128)S(1)} %get-tuple-element.37), channel_id=1, source_target_pairs={{0,2},{2,4},{4,6},{6,8},{8,10},{10,12},{12,14},{14,16},{16,18},{18... | collective-permute-start | bytes 196616 | tf_op jit(solution)/shard_map/ppermute | solution.py:15
  47.1 1.3 collective-permute-done.5
  49.8 4.2 %collective-permute-start.7 = (f32[1,4,34,1,128]{4,3,2,1,0:T(1,128)S(1)}, f32[1,4,34,1,128]{4,3,2,1,0:T(1,128)S(1)}, u32[]{:S(2)}, u32[]{:S(2)}) collective-permute-start(f32[1,4,34,1,128]{4,3,2,1,0:T(1,128)S(1)} %get-tuple-element.29), channel_id=1, source_target_pairs={{0,1},{2,3},{4,5},{6,7},{8,9},{10,11},{12,13},{14,15},{16,17},{18,... | collective-permute-start | bytes 208904 | tf_op jit(solution)/shard_map/ppermute | solution.py:15
  55.2 3.6 %select_maximum_fusion.8 = f32[1,4,34,34,130]{4,3,2,1,0:T(8,128)S(1)} fusion(f32[1,4,34,1,128]{4,3,2,1,0:T(1,128)S(1)} %collective-permute-done.6, f32[1,4,34,1,128]{4,3,2,1,0:T(1,128)S(1)} %collective-permute-done.7, f32[1,4,1,32,128]{4,3,2,1,0:T(8,128)S(1)} %collective-permute-done.4, f32[1,4,32,32,128]{4,3,2,1,0:T(8,128)S(1)} %bitcast.25, ...), kind=kLoop, calls=%fused_computation.10 | loop fusion | flops 7213440 | bytes 4771968 | tf_op jit(solution)/shard_map/concatenate | solution.py:19
  58.7 3.0 %pad_maximum_fusion = (f32[1,4,34,33,128]{4,3,2,1,0:T(8,128)}, f32[1,4,34,33,128]{4,3,2,1,0:T(8,128)}) fusion(f32[1,4,34,1,128]{4,3,2,1,0:T(1,128)S(1)} %collective-permute-done.6, f32[1,4,1,32,128]{4,3,2,1,0:T(8,128)S(1)} %collective-permute-done.4, f32[1,4,32,32,128]{4,3,2,1,0:T(8,128)S(1)} %bitcast.26, ...), kind=kLoop, calls=%fused_computation.25 | loop fusion | flops 3446784 | bytes 6963200 | tf_op jit(solution)/shard_map/concatenate | solution.py:19
  61.7 11.2 %add_subtract_fusion.2 = (f32[1,4,32,32,128]{4,3,2,1,0:T(8,128)}, f32[1,4,32,32,128]{4,3,2,1,0:T(8,128)}) fusion(f32[1,4,32,32,128]{4,3,2,1,0:T(8,128)S(1)} %bitcast.27, f32[1,4,1,32,128]{4,3,2,1,0:T(8,128)S(1)} %collective-permute-done.5, f32[1,4,1,32,128]{4,3,2,1,0:T(8,128)S(1)} %collective-permute-done.4, f32[1,4,34,33,128]{4,3,2,1,0:T(8,128)} %get-tuple-element.27, ...), kind=kLoop, calls=%fused_computation.139 | loop fusion | flops 17301504 | bytes 43122688 | tf_op jit(solution)/shard_map/sub | solution.py:73
  72.9 3.0 %add_bitcast_fusion.5 = (f32[1,2,1,32,32,128]{5,4,3,1,2,0:T(8,128)S(1)}, f32[1,2,1,32,32,128]{5,4,3,1,2,0:T(8,128)S(1)}) fusion(f32[1,4,32,32,128]{4,3,2,1,0:T(8,128)} %get-tuple-element.7, f32[1,4,32,32,128]{4,3,2,1,0:T(8,128)} %get-tuple-element.6, f32[1,4,32,32,128]{4,3,2,1,0:T(8,128)S(1)} %bitcast.28, f32[1,4,32,32,128]{4,3,2,1,0:T(8,128)S(1)} %copy-done.2, ...), kind=kLoop, calls=%fused_computation.146 | loop fusion | flops 3407872 | bytes 9961472 | tf_op jit(solution)/shard_map/stack | solution.py:80
  77.6 4.3 %collective-permute-start.9 = (f32[1,4,1,32,128]{4,3,2,1,0:T(8,128)S(1)}, f32[1,4,1,32,128]{4,3,2,1,0:T(8,128)S(1)}, u32[]{:S(2)}, u32[]{:S(2)}) collective-permute-start(f32[1,4,1,32,128]{4,3,2,1,0:T(8,128)S(1)} %get-tuple-element.35), channel_id=1, source_target_pairs={{0,2},{2,4},{4,6},{6,8},{8,10},{10,12},{12,14},{14,16},{16,18},{18... | collective-permute-start | bytes 196616 | tf_op jit(solution)/shard_map/ppermute | solution.py:15
  81.9 1.3 collective-permute-done.9
  84.6 4.0 %collective-permute-start.11 = (f32[1,4,34,1,128]{4,3,2,1,0:T(1,128)S(1)}, f32[1,4,34,1,128]{4,3,2,1,0:T(1,128)S(1)}, u32[]{:S(2)}, u32[]{:S(2)}) collective-permute-start(f32[1,4,34,1,128]{4,3,2,1,0:T(1,128)S(1)} %get-tuple-element.25), channel_id=1, source_target_pairs={{0,1},{2,3},{4,5},{6,7},{8,9},{10,11},{12,13},{14,15},{16,17},{18,... | collective-permute-start | bytes 208904 | tf_op jit(solution)/shard_map/ppermute | solution.py:15
  88.6 1.3 collective-permute-done.11
  89.9 3.6 %select_maximum_fusion.4 = f32[1,4,34,34,130]{4,3,2,1,0:T(8,128)S(1)} fusion(f32[1,4,34,1,128]{4,3,2,1,0:T(1,128)S(1)} %collective-permute-done.10, f32[1,4,34,1,128]{4,3,2,1,0:T(1,128)S(1)} %collective-permute-done.11, f32[1,4,1,32,128]{4,3,2,1,0:T(8,128)S(1)} %collective-permute-done.8, f32[1,4,32,32,128]{4,3,2,1,0:T(8,128)S(1)} %bitcast.33, ...), kind=kLoop, calls=%fused_computation.6 | loop fusion | flops 7213440 | bytes 4771968 | tf_op jit(solution)/shard_map/concatenate | solution.py:19
  93.5 3.0 %pad_maximum_fusion.1 = (f32[1,4,34,33,128]{4,3,2,1,0:T(8,128)}, f32[1,4,34,33,128]{4,3,2,1,0:T(8,128)}) fusion(f32[1,4,34,1,128]{4,3,2,1,0:T(1,128)S(1)} %collective-permute-done.10, f32[1,4,1,32,128]{4,3,2,1,0:T(8,128)S(1)} %collective-permute-done.8, f32[1,4,32,32,128]{4,3,2,1,0:T(8,128)S(1)} %bitcast.34, ...), kind=kLoop, calls=%fused_computation.27 | loop fusion | flops 3446784 | bytes 6963200 | tf_op jit(solution)/shard_map/concatenate | solution.py:19
  96.5 11.2 %add_subtract_fusion.1 = (f32[1,4,32,32,128]{4,3,2,1,0:T(8,128)}, f32[1,4,32,32,128]{4,3,2,1,0:T(8,128)}) fusion(f32[1,4,32,32,128]{4,3,2,1,0:T(8,128)S(1)} %bitcast.35, f32[1,4,1,32,128]{4,3,2,1,0:T(8,128)S(1)} %collective-permute-done.9, f32[1,4,1,32,128]{4,3,2,1,0:T(8,128)S(1)} %collective-permute-done.8, f32[1,4,34,33,128]{4,3,2,1,0:T(8,128)} %get-tuple-element.23, ...), kind=kLoop, calls=%fused_computation.138 | loop fusion | flops 17301504 | bytes 43122688 | tf_op jit(solution)/shard_map/sub | solution.py:73
  107.7 3.0 %add_bitcast_fusion.3 = (f32[1,2,1,32,32,128]{5,4,3,1,2,0:T(8,128)S(1)}, f32[1,2,1,32,32,128]{5,4,3,1,2,0:T(8,128)S(1)}) fusion(f32[1,4,32,32,128]{4,3,2,1,0:T(8,128)} %get-tuple-element.5, f32[1,4,32,32,128]{4,3,2,1,0:T(8,128)} %get-tuple-element.4, f32[1,4,32,32,128]{4,3,2,1,0:T(8,128)S(1)} %bitcast.36, f32[1,4,32,32,128]{4,3,2,1,0:T(8,128)S(1)} %bitcast.29, ...), kind=kLoop, calls=%fused_computation.144 | loop fusion | flops 3407872 | bytes 9961472 | tf_op jit(solution)/shard_map/stack | solution.py:80
  112.4 4.5 %collective-permute-start.13 = (f32[1,4,1,32,128]{4,3,2,1,0:T(8,128)S(1)}, f32[1,4,1,32,128]{4,3,2,1,0:T(8,128)S(1)}, u32[]{:S(2)}, u32[]{:S(2)}) collective-permute-start(f32[1,4,1,32,128]{4,3,2,1,0:T(8,128)S(1)} %get-tuple-element.33), channel_id=1, source_target_pairs={{0,2},{2,4},{4,6},{6,8},{8,10},{10,12},{12,14},{14,16},{16,18},{18... | collective-permute-start | bytes 196616 | tf_op jit(solution)/shard_map/ppermute | solution.py:15
  119.7 4.0 %collective-permute-start.15 = (f32[1,4,34,1,128]{4,3,2,1,0:T(1,128)S(1)}, f32[1,4,34,1,128]{4,3,2,1,0:T(1,128)S(1)}, u32[]{:S(2)}, u32[]{:S(2)}) collective-permute-start(f32[1,4,34,1,128]{4,3,2,1,0:T(1,128)S(1)} %get-tuple-element.21), channel_id=1, source_target_pairs={{0,1},{2,3},{4,5},{6,7},{8,9},{10,11},{12,13},{14,15},{16,17},{18,... | collective-permute-start | bytes 208904 | tf_op jit(solution)/shard_map/ppermute | solution.py:15
  125.0 3.6 %select_maximum_fusion = f32[1,4,34,34,130]{4,3,2,1,0:T(8,128)S(1)} fusion(f32[1,4,34,1,128]{4,3,2,1,0:T(1,128)S(1)} %collective-permute-done.14, f32[1,4,34,1,128]{4,3,2,1,0:T(1,128)S(1)} %collective-permute-done.15, f32[1,4,1,32,128]{4,3,2,1,0:T(8,128)S(1)} %collective-permute-done.12, f32[1,4,32,32,128]{4,3,2,1,0:T(8,128)S(1)} %bitcast.41, ...), kind=kLoop, calls=%fused_computation.2 | loop fusion | flops 7213440 | bytes 4771968 | tf_op jit(solution)/shard_map/concatenate | solution.py:19
  128.6 3.0 %pad_maximum_fusion.2 = (f32[1,4,34,33,128]{4,3,2,1,0:T(8,128)}, f32[1,4,34,33,128]{4,3,2,1,0:T(8,128)}) fusion(f32[1,4,34,1,128]{4,3,2,1,0:T(1,128)S(1)} %collective-permute-done.14, f32[1,4,1,32,128]{4,3,2,1,0:T(8,128)S(1)} %collective-permute-done.12, f32[1,4,32,32,128]{4,3,2,1,0:T(8,128)S(1)} %bitcast.42, ...), kind=kLoop, calls=%fused_computation.29 | loop fusion | flops 3446784 | bytes 6963200 | tf_op jit(solution)/shard_map/concatenate | solution.py:19
  131.6 13.1 %add_subtract_fusion = (f32[1,4,32,32,128]{4,3,2,1,0:T(8,128)}, f32[1,4,32,32,128]{4,3,2,1,0:T(8,128)}) fusion(f32[1,4,32,32,128]{4,3,2,1,0:T(8,128)} %bitcast.43, f32[1,4,1,32,128]{4,3,2,1,0:T(8,128)S(1)} %collective-permute-done.13, f32[1,4,1,32,128]{4,3,2,1,0:T(8,128)S(1)} %collective-permute-done.12, f32[1,4,34,33,128]{4,3,2,1,0:T(8,128)} %get-tuple-element.19, ...), kind=kLoop, calls=%fused_computation.137 | loop fusion | flops 17301504 | bytes 43122688 | tf_op jit(solution)/shard_map/sub | solution.py:73
  144.7 3.6 %add_bitcast_fusion.1 = (f32[1,2,1,32,32,128]{5,4,3,1,2,0:T(8,128)S(1)}, f32[1,2,1,32,32,128]{5,4,3,1,2,0:T(8,128)S(1)}) fusion(f32[1,4,32,32,128]{4,3,2,1,0:T(8,128)} %bitcast.44, f32[1,4,32,32,128]{4,3,2,1,0:T(8,128)} %get-tuple-element.3, f32[1,4,32,32,128]{4,3,2,1,0:T(8,128)} %get-tuple-element.2, f32[1,4,32,32,128]{4,3,2,1,0:T(8,128)S(1)} %bitcast.37, ...), kind=kLoop, calls=%fused_computation.142 | loop fusion | flops 3407872 | bytes 9961472 | tf_op jit(solution)/shard_map/stack | solution.py:80
  148.7 1.3 copy-done.12
  152.1 61.6 %all-reduce.6.cloned.1.call-done = f32[32,32,128]{2,1,0:T(8,128)} async-done(((f32[32,32,128]{2,1,0:T(8,128)}), f32[32,32,128]{2,1,0:T(8,128)}) %all-reduce.6.cloned.1.call-update) | async-done | bytes 524304 | tf_op jit(solution)/shard_map/psum | solution.py:97
  213.7 1.9 broadcast_multiply_fusion
  (71 shorter events, 17.4 us)
Async XLA Ops:
  7.2 206.6 %all-reduce.6.cloned.1.call-start = ((), (), s32[]{:S(2)}) async-start(), calls=%async_computation | async-start | bytes 1048576 | tf_op jit(solution)/shard_map/psum | solution.py:97
  8.1 11.6 %collective-permute-start.1 = (f32[1,4,1,32,128]{4,3,2,1,0:T(8,128)S(1)}, f32[1,4,1,32,128]{4,3,2,1,0:T(8,128)S(1)}, u32[]{:S(2)}, u32[]{:S(2)}) collective-permute-start(f32[1,4,1,32,128]{4,3,2,1,0:T(8,128)S(1)} %get-tuple-element.39), channel_id=1, source_target_pairs={{0,2},{2,4},{4,6},{6,8},{8,10},{10,12},{12,14},{14,16},{16,18},{18... | collective-permute-start | bytes 196616 | tf_op jit(solution)/shard_map/ppermute | solution.py:15
  12.1 7.6 %copy-start.2 = (f32[1,4,32,32,128]{4,3,2,1,0:T(8,128)S(1)}, f32[1,4,32,32,128]{4,3,2,1,0:T(8,128)}, u32[]{:S(2)}) copy-start(f32[1,4,32,32,128]{4,3,2,1,0:T(8,128)} %param.8) | copy-start | bytes 6291460
  12.2 7.9 %collective-permute-start = (f32[1,4,1,32,128]{4,3,2,1,0:T(8,128)S(1)}, f32[1,4,1,32,128]{4,3,2,1,0:T(8,128)S(1)}, u32[]{:S(2)}, u32[]{:S(2)}) collective-permute-start(f32[1,4,1,32,128]{4,3,2,1,0:T(8,128)S(1)} %get-tuple-element.38), channel_id=1, source_target_pairs={{2,0},{4,2},{6,4},{8,6},{10,8},{12,10},{14,12},{16,14},{18,16},{20... | collective-permute-start | bytes 196616 | tf_op jit(solution)/shard_map/ppermute | solution.py:18
  19.7 10.0 %copy-start.3 = (f32[32,32,128]{2,1,0:T(8,128)}, f32[32,32,128]{2,1,0:T(8,128)S(1)}, u32[]{:S(2)}) copy-start(f32[32,32,128]{2,1,0:T(8,128)S(1)} %get-tuple-element.40) | copy-start | bytes 1572868
  19.7 10.0 %copy-start.4 = (f32[32,32,128]{2,1,0:T(8,128)}, f32[32,32,128]{2,1,0:T(8,128)S(1)}, u32[]{:S(2)}) copy-start(f32[32,32,128]{2,1,0:T(8,128)S(1)} %get-tuple-element.41) | copy-start | bytes 1572868
  19.7 10.0 %copy-start.5 = (f32[32,32,128]{2,1,0:T(8,128)}, f32[32,32,128]{2,1,0:T(8,128)S(1)}, u32[]{:S(2)}) copy-start(f32[32,32,128]{2,1,0:T(8,128)S(1)} %get-tuple-element.42) | copy-start | bytes 1572868
  19.7 10.0 %copy-start.6 = (f32[32,32,128]{2,1,0:T(8,128)}, f32[32,32,128]{2,1,0:T(8,128)S(1)}, u32[]{:S(2)}) copy-start(f32[32,32,128]{2,1,0:T(8,128)S(1)} %get-tuple-element.43) | copy-start | bytes 1572868
  19.7 10.0 %copy-start.7 = (f32[32,32,128]{2,1,0:T(8,128)}, f32[32,32,128]{2,1,0:T(8,128)S(1)}, u32[]{:S(2)}) copy-start(f32[32,32,128]{2,1,0:T(8,128)S(1)} %get-tuple-element.44) | copy-start | bytes 1572868
  19.7 10.0 %copy-start.8 = (f32[32,32,128]{2,1,0:T(8,128)}, f32[32,32,128]{2,1,0:T(8,128)S(1)}, u32[]{:S(2)}) copy-start(f32[32,32,128]{2,1,0:T(8,128)S(1)} %get-tuple-element.45) | copy-start | bytes 1572868
  19.8 5.8 %copy-start.13 = (f32[32,32,128]{2,1,0:T(8,128)S(1)}, f32[32,32,128]{2,1,0:T(8,128)}, u32[]{:S(2)}) copy-start(f32[32,32,128]{2,1,0:T(8,128)} %param.12) | copy-start | bytes 1572868
  19.8 5.8 %copy-start.14 = (f32[32,32,128]{2,1,0:T(8,128)S(1)}, f32[32,32,128]{2,1,0:T(8,128)}, u32[]{:S(2)}) copy-start(f32[32,32,128]{2,1,0:T(8,128)} %param.11) | copy-start | bytes 1572868
  20.1 5.7 %collective-permute-start.2 = (f32[1,4,34,1,128]{4,3,2,1,0:T(1,128)S(1)}, f32[1,4,34,1,128]{4,3,2,1,0:T(1,128)S(1)}, u32[]{:S(2)}, u32[]{:S(2)}) collective-permute-start(f32[1,4,34,1,128]{4,3,2,1,0:T(1,128)S(1)} %get-tuple-element.31), channel_id=1, source_target_pairs={{1,0},{3,2},{5,4},{7,6},{9,8},{11,10},{13,12},{15,14},{17,16},{19,... | collective-permute-start | bytes 208904 | tf_op jit(solution)/shard_map/ppermute | solution.py:18
  21.6 5.3 %collective-permute-start.3 = (f32[1,4,34,1,128]{4,3,2,1,0:T(1,128)S(1)}, f32[1,4,34,1,128]{4,3,2,1,0:T(1,128)S(1)}, u32[]{:S(2)}, u32[]{:S(2)}) collective-permute-start(f32[1,4,34,1,128]{4,3,2,1,0:T(1,128)S(1)} %get-tuple-element.30), channel_id=1, source_target_pairs={{0,1},{2,3},{4,5},{6,7},{8,9},{10,11},{12,13},{14,15},{16,17},{18,... | collective-permute-start | bytes 208904 | tf_op jit(solution)/shard_map/ppermute | solution.py:15
  25.8 12.4 %copy-start.9 = (f32[32,32,128]{2,1,0:T(8,128)}, f32[32,32,128]{2,1,0:T(8,128)S(1)}, u32[]{:S(2)}) copy-start(f32[32,32,128]{2,1,0:T(8,128)S(1)} %get-tuple-element.46) | copy-start | bytes 1572868
  25.8 12.4 %copy-start.10 = (f32[32,32,128]{2,1,0:T(8,128)}, f32[32,32,128]{2,1,0:T(8,128)S(1)}, u32[]{:S(2)}) copy-start(f32[32,32,128]{2,1,0:T(8,128)S(1)} %get-tuple-element.47) | copy-start | bytes 1572868
  29.7 8.5 %copy-start.11 = (f32[32,32,128]{2,1,0:T(8,128)S(1)}, f32[32,32,128]{2,1,0:T(8,128)}, u32[]{:S(2)}) copy-start(f32[32,32,128]{2,1,0:T(8,128)} %param.10) | copy-start | bytes 1572868
  41.2 5.9 %collective-permute-start.4 = (f32[1,4,1,32,128]{4,3,2,1,0:T(8,128)S(1)}, f32[1,4,1,32,128]{4,3,2,1,0:T(8,128)S(1)}, u32[]{:S(2)}, u32[]{:S(2)}) collective-permute-start(f32[1,4,1,32,128]{4,3,2,1,0:T(8,128)S(1)} %get-tuple-element.36), channel_id=1, source_target_pairs={{2,0},{4,2},{6,4},{8,6},{10,8},{12,10},{14,12},{16,14},{18,16},{20... | collective-permute-start | bytes 196616 | tf_op jit(solution)/shard_map/ppermute | solution.py:18
  42.5 5.9 %collective-permute-start.5 = (f32[1,4,1,32,128]{4,3,2,1,0:T(8,128)S(1)}, f32[1,4,1,32,128]{4,3,2,1,0:T(8,128)S(1)}, u32[]{:S(2)}, u32[]{:S(2)}) collective-permute-start(f32[1,4,1,32,128]{4,3,2,1,0:T(8,128)S(1)} %get-tuple-element.37), channel_id=1, source_target_pairs={{0,2},{2,4},{4,6},{6,8},{8,10},{10,12},{12,14},{14,16},{16,18},{18... | collective-permute-start | bytes 196616 | tf_op jit(solution)/shard_map/ppermute | solution.py:15
  48.5 5.5 %collective-permute-start.6 = (f32[1,4,34,1,128]{4,3,2,1,0:T(1,128)S(1)}, f32[1,4,34,1,128]{4,3,2,1,0:T(1,128)S(1)}, u32[]{:S(2)}, u32[]{:S(2)}) collective-permute-start(f32[1,4,34,1,128]{4,3,2,1,0:T(1,128)S(1)} %get-tuple-element.28), channel_id=1, source_target_pairs={{1,0},{3,2},{5,4},{7,6},{9,8},{11,10},{13,12},{15,14},{17,16},{19,... | collective-permute-start | bytes 208904 | tf_op jit(solution)/shard_map/ppermute | solution.py:18
  49.8 5.3 %collective-permute-start.7 = (f32[1,4,34,1,128]{4,3,2,1,0:T(1,128)S(1)}, f32[1,4,34,1,128]{4,3,2,1,0:T(1,128)S(1)}, u32[]{:S(2)}, u32[]{:S(2)}) collective-permute-start(f32[1,4,34,1,128]{4,3,2,1,0:T(1,128)S(1)} %get-tuple-element.29), channel_id=1, source_target_pairs={{0,1},{2,3},{4,5},{6,7},{8,9},{10,11},{12,13},{14,15},{16,17},{18,... | collective-permute-start | bytes 208904 | tf_op jit(solution)/shard_map/ppermute | solution.py:15
  76.3 5.6 %collective-permute-start.8 = (f32[1,4,1,32,128]{4,3,2,1,0:T(8,128)S(1)}, f32[1,4,1,32,128]{4,3,2,1,0:T(8,128)S(1)}, u32[]{:S(2)}, u32[]{:S(2)}) collective-permute-start(f32[1,4,1,32,128]{4,3,2,1,0:T(8,128)S(1)} %get-tuple-element.34), channel_id=1, source_target_pairs={{2,0},{4,2},{6,4},{8,6},{10,8},{12,10},{14,12},{16,14},{18,16},{20... | collective-permute-start | bytes 196616 | tf_op jit(solution)/shard_map/ppermute | solution.py:18
  77.6 5.6 %collective-permute-start.9 = (f32[1,4,1,32,128]{4,3,2,1,0:T(8,128)S(1)}, f32[1,4,1,32,128]{4,3,2,1,0:T(8,128)S(1)}, u32[]{:S(2)}, u32[]{:S(2)}) collective-permute-start(f32[1,4,1,32,128]{4,3,2,1,0:T(8,128)S(1)} %get-tuple-element.35), channel_id=1, source_target_pairs={{0,2},{2,4},{4,6},{6,8},{8,10},{10,12},{12,14},{14,16},{16,18},{18... | collective-permute-start | bytes 196616 | tf_op jit(solution)/shard_map/ppermute | solution.py:15
  83.3 5.3 %collective-permute-start.10 = (f32[1,4,34,1,128]{4,3,2,1,0:T(1,128)S(1)}, f32[1,4,34,1,128]{4,3,2,1,0:T(1,128)S(1)}, u32[]{:S(2)}, u32[]{:S(2)}) collective-permute-start(f32[1,4,34,1,128]{4,3,2,1,0:T(1,128)S(1)} %get-tuple-element.24), channel_id=1, source_target_pairs={{1,0},{3,2},{5,4},{7,6},{9,8},{11,10},{13,12},{15,14},{17,16},{19,... | collective-permute-start | bytes 208904 | tf_op jit(solution)/shard_map/ppermute | solution.py:18
  84.6 5.3 %collective-permute-start.11 = (f32[1,4,34,1,128]{4,3,2,1,0:T(1,128)S(1)}, f32[1,4,34,1,128]{4,3,2,1,0:T(1,128)S(1)}, u32[]{:S(2)}, u32[]{:S(2)}) collective-permute-start(f32[1,4,34,1,128]{4,3,2,1,0:T(1,128)S(1)} %get-tuple-element.25), channel_id=1, source_target_pairs={{0,1},{2,3},{4,5},{6,7},{8,9},{10,11},{12,13},{14,15},{16,17},{18,... | collective-permute-start | bytes 208904 | tf_op jit(solution)/shard_map/ppermute | solution.py:15
  111.1 17.5 %copy-start = (f32[1,2,2,32,32,128]{5,4,3,2,1,0:T(8,128)}, f32[1,2,2,32,32,128]{5,4,3,2,1,0:T(8,128)S(1)}, u32[]{:S(2)}) copy-start(f32[1,2,2,32,32,128]{5,4,3,2,1,0:T(8,128)S(1)} %copy.14) | copy-start | bytes 6291460
  111.1 5.9 %collective-permute-start.12 = (f32[1,4,1,32,128]{4,3,2,1,0:T(8,128)S(1)}, f32[1,4,1,32,128]{4,3,2,1,0:T(8,128)S(1)}, u32[]{:S(2)}, u32[]{:S(2)}) collective-permute-start(f32[1,4,1,32,128]{4,3,2,1,0:T(8,128)S(1)} %get-tuple-element.32), channel_id=1, source_target_pairs={{2,0},{4,2},{6,4},{8,6},{10,8},{12,10},{14,12},{16,14},{18,16},{20... | collective-permute-start | bytes 196616 | tf_op jit(solution)/shard_map/ppermute | solution.py:18
  112.4 5.9 %collective-permute-start.13 = (f32[1,4,1,32,128]{4,3,2,1,0:T(8,128)S(1)}, f32[1,4,1,32,128]{4,3,2,1,0:T(8,128)S(1)}, u32[]{:S(2)}, u32[]{:S(2)}) collective-permute-start(f32[1,4,1,32,128]{4,3,2,1,0:T(8,128)S(1)} %get-tuple-element.33), channel_id=1, source_target_pairs={{0,2},{2,4},{4,6},{6,8},{8,10},{10,12},{12,14},{14,16},{16,18},{18... | collective-permute-start | bytes 196616 | tf_op jit(solution)/shard_map/ppermute | solution.py:15
  118.4 5.9 %collective-permute-start.14 = (f32[1,4,34,1,128]{4,3,2,1,0:T(1,128)S(1)}, f32[1,4,34,1,128]{4,3,2,1,0:T(1,128)S(1)}, u32[]{:S(2)}, u32[]{:S(2)}) collective-permute-start(f32[1,4,34,1,128]{4,3,2,1,0:T(1,128)S(1)} %get-tuple-element.20), channel_id=1, source_target_pairs={{1,0},{3,2},{5,4},{7,6},{9,8},{11,10},{13,12},{15,14},{17,16},{19,... | collective-permute-start | bytes 208904 | tf_op jit(solution)/shard_map/ppermute | solution.py:18
  119.7 5.3 %collective-permute-start.15 = (f32[1,4,34,1,128]{4,3,2,1,0:T(1,128)S(1)}, f32[1,4,34,1,128]{4,3,2,1,0:T(1,128)S(1)}, u32[]{:S(2)}, u32[]{:S(2)}) collective-permute-start(f32[1,4,34,1,128]{4,3,2,1,0:T(1,128)S(1)} %get-tuple-element.21), channel_id=1, source_target_pairs={{0,1},{2,3},{4,5},{6,7},{8,9},{10,11},{12,13},{14,15},{16,17},{18,... | collective-permute-start | bytes 208904 | tf_op jit(solution)/shard_map/ppermute | solution.py:15
  148.5 2.3 %copy-start.1 = (f32[1,2,2,32,32,128]{5,4,3,2,1,0:T(8,128)S(1)}, f32[1,2,2,32,32,128]{5,4,3,2,1,0:T(8,128)}, u32[]{:S(2)}) copy-start(f32[1,2,2,32,32,128]{5,4,3,2,1,0:T(8,128)} %copy-done) | copy-start | bytes 6291460
  148.6 1.3 copy-start.12
Sparse Core Ops, SparseCore 0:
  152.2 61.4 all-reduce.5
where the time goes:
time: 223 us; the launch traced here: 222 us
  other arithmetic  88.9 us (40%)
  waiting for transfers between devices  69.8 us (31%)
  starting transfers between devices  44.3 us (20%)
  between operations  15.3 us (7%)
  local copies, waits for them, and re-layouts  4.16 us (2%)
    psum x1, waiting for transfers between devices, local(): image = lax.psum(covered * correlation, 'shot') / ITERS  61.6 us
    sub x4, other arithmetic, advance(): across = second_x + second_y + second_z - along  44 us
    ppermute x8, starting transfers between devices, extended(): lax.ppermute(lax.slice_in_dim(block, block.shape[dim] - width, None, axis...  33.6 us
    concatenate x7, other arithmetic, extended(): block = jnp.concatenate([low, block, high], axis=dim)  22.4 us
    another operation x8, other arithmetic, advance(): return jnp.stack([next_p, next_q], axis=2).reshape(centre.shape)  12.8 us
    ppermute x8, starting transfers between devices, extended(): lax.ppermute(lax.slice_in_dim(block, 0, width, axis=dim), axis, backward)  10.6 us
    ppermute x8, waiting for transfers between devices, extended(): lax.ppermute(lax.slice_in_dim(block, block.shape[dim] - width, None, axis...  8.18 us
    mul x1, other arithmetic, advance(): normal_x * normal_x * second_x + normal_y * normal_y * second_y  6.06 us
  transfers between devices with their start and end apart: 17, of which 8 were waited for; matrix products, arithmetic and copies ran while one was open for 3% of the time, Pallas kernels for 0%

commit v1 on v0

--- a/solution.py
+++ b/solution.py
@@ -5,6 +5,12 @@
 from jax.sharding import PartitionSpec as P
 
 ITERS = 4
+
+
+def gather_and_add(x, axis):
+    parts = lax.all_gather(x, axis, axis=0, tiled=False)
+    result = parts.sum(axis=0)
+    return result
 
 
 def extended(block, sides, width):
@@ -94,7 +100,7 @@
         correlation = correlation + fresh[0, 0] * fresh[0, 2]
         previous, current = (current, fresh)
     covered = aperture[0, 0, 0].astype(jnp.float32)
-    image = lax.psum(covered * correlation, "shot") / ITERS
+    image = gather_and_add(covered * correlation, "shot") / ITERS
     return (current, image)
 
 

time: 223 us -> 209 us (0.937)
  waiting for transfers between devices: 69.8 us -> 54.4 us
    psum x1 -> x0, waiting for transfers between devices: 61.6 us -> none  [local(): image = lax.psum(covered * correlation, 'shot') / ITERS]
    all_gather x0 -> x1, waiting for transfers between devices: none -> 46.2 us  [gather_and_add(): parts = lax.all_gather(x, axis, axis=0, tiled=False)]
where the time goes in v1:
time: 209 us; the launch traced here: 208 us
  other arithmetic  89.7 us (43%)
  waiting for transfers between devices  54.4 us (26%)
  starting transfers between devices  44.3 us (21%)
  between operations  15.3 us (7%)
  local copies, waits for them, and re-layouts  4.16 us (2%)
    all_gather x1, waiting for transfers between devices, gather_and_add(): parts = lax.all_gather(x, axis, axis=0, tiled=False)  46.2 us
    sub x4, other arithmetic, advance(): across = second_x + second_y + second_z - along  44 us
    ppermute x8, starting transfers between devices, extended(): lax.ppermute(lax.slice_in_dim(block, block.shape[dim] - width, None, axis...  33.6 us
    concatenate x7, other arithmetic, extended(): block = jnp.concatenate([low, block, high], axis=dim)  22.4 us
    another operation x8, other arithmetic, advance(): return jnp.stack([next_p, next_q], axis=2).reshape(centre.shape)  12.8 us
    ppermute x8, starting transfers between devices, extended(): lax.ppermute(lax.slice_in_dim(block, 0, width, axis=dim), axis, backward)  10.6 us
    ppermute x8, waiting for transfers between devices, extended(): lax.ppermute(lax.slice_in_dim(block, block.shape[dim] - width, None, axis...  8.18 us
    mul x1, other arithmetic, advance(): normal_x * normal_x * second_x + normal_y * normal_y * second_y  6.06 us
  transfers between devices with their start and end apart: 17, of which 8 were waited for; matrix products, arithmetic and copies ran while one was open for 3% of the time, Pallas kernels for 0%

profile of v1, /device:TPU:1, one launch (start us, length us, event | category | flops | bytes accessed | tf_op | source)
XLA Modules:
  0.0 207.9 jit_solution(9468310593393684555)
XLA Ops:
  8.1 4.0 %collective-permute-start.1 = (f32[1,4,1,32,128]{4,3,2,1,0:T(8,128)S(1)}, f32[1,4,1,32,128]{4,3,2,1,0:T(8,128)S(1)}, u32[]{:S(2)}, u32[]{:S(2)}) collective-permute-start(f32[1,4,1,32,128]{4,3,2,1,0:T(8,128)S(1)} %get-tuple-element.39), channel_id=1, source_target_pairs={{0,2},{2,4},{4,6},{6,8},{8,10},{10,12},{12,14},{14,16},{16,18},{18... | collective-permute-start | bytes 196616 | tf_op jit(solution)/shard_map/ppermute | solution.py:21
  12.2 1.4 collective-permute-start
  13.6 6.1 %fusion.60 = (f32[32,32,128]{2,1,0:T(8,128)S(1)}, f32[32,32,128]{2,1,0:T(8,128)S(1)}, f32[32,32,128]{2,1,0:T(8,128)S(1)}, f32[32,32,128]{2,1,0:T(8,128)S(1)}, f3...) fusion(s32[32,32,128]{2,1,0:T(8,128)} %param.14, s32[32,32,128]{2,1,0:T(8,128)} %param.13), kind=kLoop, calls=%fused_computation.182 | loop fusion | flops 1966080 | bytes 4194304 | tf_op jit(solution)/shard_map/mul | solution.py:69
  20.1 1.4 collective-permute-start.2
  21.6 4.0 %collective-permute-start.3 = (f32[1,4,34,1,128]{4,3,2,1,0:T(1,128)S(1)}, f32[1,4,34,1,128]{4,3,2,1,0:T(1,128)S(1)}, u32[]{:S(2)}, u32[]{:S(2)}) collective-permute-start(f32[1,4,34,1,128]{4,3,2,1,0:T(1,128)S(1)} %get-tuple-element.30), channel_id=1, source_target_pairs={{0,1},{2,3},{4,5},{6,7},{8,9},{10,11},{12,13},{14,15},{16,17},{18,... | collective-permute-start | bytes 208904 | tf_op jit(solution)/shard_map/ppermute | solution.py:21
  26.9 2.7 %select_maximum_fusion.12 = f32[1,4,34,34,130]{4,3,2,1,0:T(8,128)S(1)} fusion(f32[1,4,34,1,128]{4,3,2,1,0:T(1,128)S(1)} %collective-permute-done.2, f32[1,4,34,32,128]{4,3,2,1,0:T(8,128)S(1)} %constant_dynamic-update-slice_fusion, f32[1,4,34,1,128]{4,3,2,1,0:T(1,128)S(1)} %collective-permute-done.3), kind=kLoop, calls=%fused_computation.14 | loop fusion | flops 4808960 | bytes 4771968 | tf_op jit(solution)/shard_map/concatenate | solution.py:25
  29.7 8.4 %add_subtract_fusion.3 = (f32[1,4,32,32,128]{4,3,2,1,0:T(8,128)S(1)}, f32[1,4,32,32,128]{4,3,2,1,0:T(8,128)S(1)}) fusion(f32[1,4,32,32,128]{4,3,2,1,0:T(8,128)S(1)} %copy-done.2, f32[1,4,1,32,128]{4,3,2,1,0:T(8,128)S(1)} %collective-permute-done.1, f32[1,4,1,32,128]{4,3,2,1,0:T(8,128)S(1)} %collective-permute-done, ...), kind=kLoop, calls=%fused_computation.140 | loop fusion | flops 22544384 | bytes 32907264 | tf_op jit(solution)/shard_map/sub | solution.py:79
  38.2 2.5 %add_bitcast_fusion.7 = (f32[1,2,1,32,32,128]{5,4,3,1,2,0:T(8,128)S(1)}, f32[1,2,1,32,32,128]{5,4,3,1,2,0:T(8,128)S(1)}) fusion(f32[1,4,32,32,128]{4,3,2,1,0:T(8,128)} %param.9, f32[1,4,32,32,128]{4,3,2,1,0:T(8,128)S(1)} %get-tuple-element.9, f32[1,4,32,32,128]{4,3,2,1,0:T(8,128)S(1)} %get-tuple-element.8, f32[1,4,32,32,128]{4,3,2,1,0:T(8,128)S(1)} %copy-done.2, ...), kind=kLoop, calls=%fused_computation.148 | loop fusion | flops 3407872 | bytes 9961472 | tf_op jit(solution)/shard_map/stack | solution.py:86
  42.5 4.6 %collective-permute-start.5 = (f32[1,4,1,32,128]{4,3,2,1,0:T(8,128)S(1)}, f32[1,4,1,32,128]{4,3,2,1,0:T(8,128)S(1)}, u32[]{:S(2)}, u32[]{:S(2)}) collective-permute-start(f32[1,4,1,32,128]{4,3,2,1,0:T(8,128)S(1)} %get-tuple-element.37), channel_id=1, source_target_pairs={{0,2},{2,4},{4,6},{6,8},{8,10},{10,12},{12,14},{14,16},{16,18},{18... | collective-permute-start | bytes 196616 | tf_op jit(solution)/shard_map/ppermute | solution.py:21
  47.1 1.3 collective-permute-done.5
  49.8 4.2 %collective-permute-start.7 = (f32[1,4,34,1,128]{4,3,2,1,0:T(1,128)S(1)}, f32[1,4,34,1,128]{4,3,2,1,0:T(1,128)S(1)}, u32[]{:S(2)}, u32[]{:S(2)}) collective-permute-start(f32[1,4,34,1,128]{4,3,2,1,0:T(1,128)S(1)} %get-tuple-element.29), channel_id=1, source_target_pairs={{0,1},{2,3},{4,5},{6,7},{8,9},{10,11},{12,13},{14,15},{16,17},{18,... | collective-permute-start | bytes 208904 | tf_op jit(solution)/shard_map/ppermute | solution.py:21
  55.2 3.6 %select_maximum_fusion.8 = f32[1,4,34,34,130]{4,3,2,1,0:T(8,128)S(1)} fusion(f32[1,4,34,1,128]{4,3,2,1,0:T(1,128)S(1)} %collective-permute-done.6, f32[1,4,34,1,128]{4,3,2,1,0:T(1,128)S(1)} %collective-permute-done.7, f32[1,4,1,32,128]{4,3,2,1,0:T(8,128)S(1)} %collective-permute-done.4, f32[1,4,32,32,128]{4,3,2,1,0:T(8,128)S(1)} %bitcast.23, ...), kind=kLoop, calls=%fused_computation.10 | loop fusion | flops 7213440 | bytes 4771968 | tf_op jit(solution)/shard_map/concatenate | solution.py:25
  58.7 3.0 %pad_maximum_fusion = (f32[1,4,34,33,128]{4,3,2,1,0:T(8,128)}, f32[1,4,34,33,128]{4,3,2,1,0:T(8,128)}) fusion(f32[1,4,34,1,128]{4,3,2,1,0:T(1,128)S(1)} %collective-permute-done.6, f32[1,4,1,32,128]{4,3,2,1,0:T(8,128)S(1)} %collective-permute-done.4, f32[1,4,32,32,128]{4,3,2,1,0:T(8,128)S(1)} %bitcast.24, ...), kind=kLoop, calls=%fused_computation.25 | loop fusion | flops 3446784 | bytes 6963200 | tf_op jit(solution)/shard_map/concatenate | solution.py:25
  61.7 11.2 %add_subtract_fusion.2 = (f32[1,4,32,32,128]{4,3,2,1,0:T(8,128)}, f32[1,4,32,32,128]{4,3,2,1,0:T(8,128)}) fusion(f32[1,4,32,32,128]{4,3,2,1,0:T(8,128)S(1)} %bitcast.25, f32[1,4,1,32,128]{4,3,2,1,0:T(8,128)S(1)} %collective-permute-done.5, f32[1,4,1,32,128]{4,3,2,1,0:T(8,128)S(1)} %collective-permute-done.4, f32[1,4,34,33,128]{4,3,2,1,0:T(8,128)} %get-tuple-element.27, ...), kind=kLoop, calls=%fused_computation.139 | loop fusion | flops 17301504 | bytes 43122688 | tf_op jit(solution)/shard_map/sub | solution.py:79
  72.9 3.0 %add_bitcast_fusion.5 = (f32[1,2,1,32,32,128]{5,4,3,1,2,0:T(8,128)S(1)}, f32[1,2,1,32,32,128]{5,4,3,1,2,0:T(8,128)S(1)}) fusion(f32[1,4,32,32,128]{4,3,2,1,0:T(8,128)} %get-tuple-element.7, f32[1,4,32,32,128]{4,3,2,1,0:T(8,128)} %get-tuple-element.6, f32[1,4,32,32,128]{4,3,2,1,0:T(8,128)S(1)} %bitcast.26, f32[1,4,32,32,128]{4,3,2,1,0:T(8,128)S(1)} %copy-done.2, ...), kind=kLoop, calls=%fused_computation.146 | loop fusion | flops 3407872 | bytes 9961472 | tf_op jit(solution)/shard_map/stack | solution.py:86
  77.6 4.3 %collective-permute-start.9 = (f32[1,4,1,32,128]{4,3,2,1,0:T(8,128)S(1)}, f32[1,4,1,32,128]{4,3,2,1,0:T(8,128)S(1)}, u32[]{:S(2)}, u32[]{:S(2)}) collective-permute-start(f32[1,4,1,32,128]{4,3,2,1,0:T(8,128)S(1)} %get-tuple-element.35), channel_id=1, source_target_pairs={{0,2},{2,4},{4,6},{6,8},{8,10},{10,12},{12,14},{14,16},{16,18},{18... | collective-permute-start | bytes 196616 | tf_op jit(solution)/shard_map/ppermute | solution.py:21
  81.9 1.3 collective-permute-done.9
  84.6 4.0 %collective-permute-start.11 = (f32[1,4,34,1,128]{4,3,2,1,0:T(1,128)S(1)}, f32[1,4,34,1,128]{4,3,2,1,0:T(1,128)S(1)}, u32[]{:S(2)}, u32[]{:S(2)}) collective-permute-start(f32[1,4,34,1,128]{4,3,2,1,0:T(1,128)S(1)} %get-tuple-element.25), channel_id=1, source_target_pairs={{0,1},{2,3},{4,5},{6,7},{8,9},{10,11},{12,13},{14,15},{16,17},{18,... | collective-permute-start | bytes 208904 | tf_op jit(solution)/shard_map/ppermute | solution.py:21
  88.6 1.3 collective-permute-done.11
  89.9 3.6 %select_maximum_fusion.4 = f32[1,4,34,34,130]{4,3,2,1,0:T(8,128)S(1)} fusion(f32[1,4,34,1,128]{4,3,2,1,0:T(1,128)S(1)} %collective-permute-done.10, f32[1,4,34,1,128]{4,3,2,1,0:T(1,128)S(1)} %collective-permute-done.11, f32[1,4,1,32,128]{4,3,2,1,0:T(8,128)S(1)} %collective-permute-done.8, f32[1,4,32,32,128]{4,3,2,1,0:T(8,128)S(1)} %bitcast.31, ...), kind=kLoop, calls=%fused_computation.6 | loop fusion | flops 7213440 | bytes 4771968 | tf_op jit(solution)/shard_map/concatenate | solution.py:25
  93.5 3.0 %pad_maximum_fusion.1 = (f32[1,4,34,33,128]{4,3,2,1,0:T(8,128)}, f32[1,4,34,33,128]{4,3,2,1,0:T(8,128)}) fusion(f32[1,4,34,1,128]{4,3,2,1,0:T(1,128)S(1)} %collective-permute-done.10, f32[1,4,1,32,128]{4,3,2,1,0:T(8,128)S(1)} %collective-permute-done.8, f32[1,4,32,32,128]{4,3,2,1,0:T(8,128)S(1)} %bitcast.32, ...), kind=kLoop, calls=%fused_computation.27 | loop fusion | flops 3446784 | bytes 6963200 | tf_op jit(solution)/shard_map/concatenate | solution.py:25
  96.5 11.2 %add_subtract_fusion.1 = (f32[1,4,32,32,128]{4,3,2,1,0:T(8,128)}, f32[1,4,32,32,128]{4,3,2,1,0:T(8,128)}) fusion(f32[1,4,32,32,128]{4,3,2,1,0:T(8,128)S(1)} %bitcast.33, f32[1,4,1,32,128]{4,3,2,1,0:T(8,128)S(1)} %collective-permute-done.9, f32[1,4,1,32,128]{4,3,2,1,0:T(8,128)S(1)} %collective-permute-done.8, f32[1,4,34,33,128]{4,3,2,1,0:T(8,128)} %get-tuple-element.23, ...), kind=kLoop, calls=%fused_computation.138 | loop fusion | flops 17301504 | bytes 43122688 | tf_op jit(solution)/shard_map/sub | solution.py:79
  107.7 3.0 %add_bitcast_fusion.3 = (f32[1,2,1,32,32,128]{5,4,3,1,2,0:T(8,128)S(1)}, f32[1,2,1,32,32,128]{5,4,3,1,2,0:T(8,128)S(1)}) fusion(f32[1,4,32,32,128]{4,3,2,1,0:T(8,128)} %get-tuple-element.5, f32[1,4,32,32,128]{4,3,2,1,0:T(8,128)} %get-tuple-element.4, f32[1,4,32,32,128]{4,3,2,1,0:T(8,128)S(1)} %bitcast.34, f32[1,4,32,32,128]{4,3,2,1,0:T(8,128)S(1)} %bitcast.27, ...), kind=kLoop, calls=%fused_computation.144 | loop fusion | flops 3407872 | bytes 9961472 | tf_op jit(solution)/shard_map/stack | solution.py:86
  112.4 4.5 %collective-permute-start.13 = (f32[1,4,1,32,128]{4,3,2,1,0:T(8,128)S(1)}, f32[1,4,1,32,128]{4,3,2,1,0:T(8,128)S(1)}, u32[]{:S(2)}, u32[]{:S(2)}) collective-permute-start(f32[1,4,1,32,128]{4,3,2,1,0:T(8,128)S(1)} %get-tuple-element.33), channel_id=1, source_target_pairs={{0,2},{2,4},{4,6},{6,8},{8,10},{10,12},{12,14},{14,16},{16,18},{18... | collective-permute-start | bytes 196616 | tf_op jit(solution)/shard_map/ppermute | solution.py:21
  119.7 4.0 %collective-permute-start.15 = (f32[1,4,34,1,128]{4,3,2,1,0:T(1,128)S(1)}, f32[1,4,34,1,128]{4,3,2,1,0:T(1,128)S(1)}, u32[]{:S(2)}, u32[]{:S(2)}) collective-permute-start(f32[1,4,34,1,128]{4,3,2,1,0:T(1,128)S(1)} %get-tuple-element.21), channel_id=1, source_target_pairs={{0,1},{2,3},{4,5},{6,7},{8,9},{10,11},{12,13},{14,15},{16,17},{18,... | collective-permute-start | bytes 208904 | tf_op jit(solution)/shard_map/ppermute | solution.py:21
  125.0 3.6 %select_maximum_fusion = f32[1,4,34,34,130]{4,3,2,1,0:T(8,128)S(1)} fusion(f32[1,4,34,1,128]{4,3,2,1,0:T(1,128)S(1)} %collective-permute-done.14, f32[1,4,34,1,128]{4,3,2,1,0:T(1,128)S(1)} %collective-permute-done.15, f32[1,4,1,32,128]{4,3,2,1,0:T(8,128)S(1)} %collective-permute-done.12, f32[1,4,32,32,128]{4,3,2,1,0:T(8,128)S(1)} %bitcast.39, ...), kind=kLoop, calls=%fused_computation.2 | loop fusion | flops 7213440 | bytes 4771968 | tf_op jit(solution)/shard_map/concatenate | solution.py:25
  128.6 3.0 %pad_maximum_fusion.2 = (f32[1,4,34,33,128]{4,3,2,1,0:T(8,128)}, f32[1,4,34,33,128]{4,3,2,1,0:T(8,128)}) fusion(f32[1,4,34,1,128]{4,3,2,1,0:T(1,128)S(1)} %collective-permute-done.14, f32[1,4,1,32,128]{4,3,2,1,0:T(8,128)S(1)} %collective-permute-done.12, f32[1,4,32,32,128]{4,3,2,1,0:T(8,128)S(1)} %bitcast.40, ...), kind=kLoop, calls=%fused_computation.29 | loop fusion | flops 3446784 | bytes 6963200 | tf_op jit(solution)/shard_map/concatenate | solution.py:25
  131.6 13.1 %add_subtract_fusion = (f32[1,4,32,32,128]{4,3,2,1,0:T(8,128)}, f32[1,4,32,32,128]{4,3,2,1,0:T(8,128)}) fusion(f32[1,4,32,32,128]{4,3,2,1,0:T(8,128)} %bitcast.41, f32[1,4,1,32,128]{4,3,2,1,0:T(8,128)S(1)} %collective-permute-done.13, f32[1,4,1,32,128]{4,3,2,1,0:T(8,128)S(1)} %collective-permute-done.12, f32[1,4,34,33,128]{4,3,2,1,0:T(8,128)} %get-tuple-element.19, ...), kind=kLoop, calls=%fused_computation.137 | loop fusion | flops 17301504 | bytes 43122688 | tf_op jit(solution)/shard_map/sub | solution.py:79
  144.7 3.6 %add_bitcast_fusion.1 = (f32[1,2,1,32,32,128]{5,4,3,1,2,0:T(8,128)S(1)}, f32[1,2,1,32,32,128]{5,4,3,1,2,0:T(8,128)S(1)}) fusion(f32[1,4,32,32,128]{4,3,2,1,0:T(8,128)} %bitcast.42, f32[1,4,32,32,128]{4,3,2,1,0:T(8,128)} %get-tuple-element.3, f32[1,4,32,32,128]{4,3,2,1,0:T(8,128)} %get-tuple-element.2, f32[1,4,32,32,128]{4,3,2,1,0:T(8,128)S(1)} %bitcast.35, ...), kind=kLoop, calls=%fused_computation.142 | loop fusion | flops 3407872 | bytes 9961472 | tf_op jit(solution)/shard_map/stack | solution.py:86
  148.7 1.3 copy-done.12
  152.1 46.2 %all-gather.3.cloned.1.call-done = f32[4,1,32,32,128]{4,3,2,1,0:T(8,128)} async-done(((f32[1,1,32,32,128]{4,3,2,1,0:T(8,128)}), f32[4,1,32,32,128]{4,3,2,1,0:T(8,128)}) %all-gather.3.cloned.1.call-update) | async-done | bytes 2097168 | tf_op jit(solution)/shard_map/all_gather | solution.py:11
  198.3 1.9 reduce_sum.9
  (72 shorter events, 18.3 us)
Async XLA Ops:
  7.2 191.1 %all-gather.3.cloned.1.call-start = ((), (), s32[]{:S(2)}) async-start(), calls=%async_computation | async-start | bytes 2621440 | tf_op jit(solution)/shard_map/all_gather | solution.py:11
  8.1 11.6 %collective-permute-start.1 = (f32[1,4,1,32,128]{4,3,2,1,0:T(8,128)S(1)}, f32[1,4,1,32,128]{4,3,2,1,0:T(8,128)S(1)}, u32[]{:S(2)}, u32[]{:S(2)}) collective-permute-start(f32[1,4,1,32,128]{4,3,2,1,0:T(8,128)S(1)} %get-tuple-element.39), channel_id=1, source_target_pairs={{0,2},{2,4},{4,6},{6,8},{8,10},{10,12},{12,14},{14,16},{16,18},{18... | collective-permute-start | bytes 196616 | tf_op jit(solution)/shard_map/ppermute | solution.py:21
  12.1 7.6 %copy-start.2 = (f32[1,4,32,32,128]{4,3,2,1,0:T(8,128)S(1)}, f32[1,4,32,32,128]{4,3,2,1,0:T(8,128)}, u32[]{:S(2)}) copy-start(f32[1,4,32,32,128]{4,3,2,1,0:T(8,128)} %param.8) | copy-start | bytes 6291460
  12.2 7.9 %collective-permute-start = (f32[1,4,1,32,128]{4,3,2,1,0:T(8,128)S(1)}, f32[1,4,1,32,128]{4,3,2,1,0:T(8,128)S(1)}, u32[]{:S(2)}, u32[]{:S(2)}) collective-permute-start(f32[1,4,1,32,128]{4,3,2,1,0:T(8,128)S(1)} %get-tuple-element.38), channel_id=1, source_target_pairs={{2,0},{4,2},{6,4},{8,6},{10,8},{12,10},{14,12},{16,14},{18,16},{20... | collective-permute-start | bytes 196616 | tf_op jit(solution)/shard_map/ppermute | solution.py:24
  19.7 10.0 %copy-start.3 = (f32[32,32,128]{2,1,0:T(8,128)}, f32[32,32,128]{2,1,0:T(8,128)S(1)}, u32[]{:S(2)}) copy-start(f32[32,32,128]{2,1,0:T(8,128)S(1)} %get-tuple-element.40) | copy-start | bytes 1572868
  19.7 10.0 %copy-start.4 = (f32[32,32,128]{2,1,0:T(8,128)}, f32[32,32,128]{2,1,0:T(8,128)S(1)}, u32[]{:S(2)}) copy-start(f32[32,32,128]{2,1,0:T(8,128)S(1)} %get-tuple-element.41) | copy-start | bytes 1572868
  19.7 10.0 %copy-start.5 = (f32[32,32,128]{2,1,0:T(8,128)}, f32[32,32,128]{2,1,0:T(8,128)S(1)}, u32[]{:S(2)}) copy-start(f32[32,32,128]{2,1,0:T(8,128)S(1)} %get-tuple-element.42) | copy-start | bytes 1572868
  19.7 10.0 %copy-start.6 = (f32[32,32,128]{2,1,0:T(8,128)}, f32[32,32,128]{2,1,0:T(8,128)S(1)}, u32[]{:S(2)}) copy-start(f32[32,32,128]{2,1,0:T(8,128)S(1)} %get-tuple-element.43) | copy-start | bytes 1572868
  19.7 10.0 %copy-start.7 = (f32[32,32,128]{2,1,0:T(8,128)}, f32[32,32,128]{2,1,0:T(8,128)S(1)}, u32[]{:S(2)}) copy-start(f32[32,32,128]{2,1,0:T(8,128)S(1)} %get-tuple-element.44) | copy-start | bytes 1572868
  19.7 10.0 %copy-start.8 = (f32[32,32,128]{2,1,0:T(8,128)}, f32[32,32,128]{2,1,0:T(8,128)S(1)}, u32[]{:S(2)}) copy-start(f32[32,32,128]{2,1,0:T(8,128)S(1)} %get-tuple-element.45) | copy-start | bytes 1572868
  19.8 5.8 %copy-start.13 = (f32[32,32,128]{2,1,0:T(8,128)S(1)}, f32[32,32,128]{2,1,0:T(8,128)}, u32[]{:S(2)}) copy-start(f32[32,32,128]{2,1,0:T(8,128)} %param.12) | copy-start | bytes 1572868
  19.8 5.8 %copy-start.14 = (f32[32,32,128]{2,1,0:T(8,128)S(1)}, f32[32,32,128]{2,1,0:T(8,128)}, u32[]{:S(2)}) copy-start(f32[32,32,128]{2,1,0:T(8,128)} %param.11) | copy-start | bytes 1572868
  20.1 5.7 %collective-permute-start.2 = (f32[1,4,34,1,128]{4,3,2,1,0:T(1,128)S(1)}, f32[1,4,34,1,128]{4,3,2,1,0:T(1,128)S(1)}, u32[]{:S(2)}, u32[]{:S(2)}) collective-permute-start(f32[1,4,34,1,128]{4,3,2,1,0:T(1,128)S(1)} %get-tuple-element.31), channel_id=1, source_target_pairs={{1,0},{3,2},{5,4},{7,6},{9,8},{11,10},{13,12},{15,14},{17,16},{19,... | collective-permute-start | bytes 208904 | tf_op jit(solution)/shard_map/ppermute | solution.py:24
  21.6 5.3 %collective-permute-start.3 = (f32[1,4,34,1,128]{4,3,2,1,0:T(1,128)S(1)}, f32[1,4,34,1,128]{4,3,2,1,0:T(1,128)S(1)}, u32[]{:S(2)}, u32[]{:S(2)}) collective-permute-start(f32[1,4,34,1,128]{4,3,2,1,0:T(1,128)S(1)} %get-tuple-element.30), channel_id=1, source_target_pairs={{0,1},{2,3},{4,5},{6,7},{8,9},{10,11},{12,13},{14,15},{16,17},{18,... | collective-permute-start | bytes 208904 | tf_op jit(solution)/shard_map/ppermute | solution.py:21
  25.8 12.4 %copy-start.9 = (f32[32,32,128]{2,1,0:T(8,128)}, f32[32,32,128]{2,1,0:T(8,128)S(1)}, u32[]{:S(2)}) copy-start(f32[32,32,128]{2,1,0:T(8,128)S(1)} %get-tuple-element.46) | copy-start | bytes 1572868
  25.8 12.4 %copy-start.10 = (f32[32,32,128]{2,1,0:T(8,128)}, f32[32,32,128]{2,1,0:T(8,128)S(1)}, u32[]{:S(2)}) copy-start(f32[32,32,128]{2,1,0:T(8,128)S(1)} %get-tuple-element.47) | copy-start | bytes 1572868
  29.7 8.5 %copy-start.11 = (f32[32,32,128]{2,1,0:T(8,128)S(1)}, f32[32,32,128]{2,1,0:T(8,128)}, u32[]{:S(2)}) copy-start(f32[32,32,128]{2,1,0:T(8,128)} %param.10) | copy-start | bytes 1572868
  41.2 5.9 %collective-permute-start.4 = (f32[1,4,1,32,128]{4,3,2,1,0:T(8,128)S(1)}, f32[1,4,1,32,128]{4,3,2,1,0:T(8,128)S(1)}, u32[]{:S(2)}, u32[]{:S(2)}) collective-permute-start(f32[1,4,1,32,128]{4,3,2,1,0:T(8,128)S(1)} %get-tuple-element.36), channel_id=1, source_target_pairs={{2,0},{4,2},{6,4},{8,6},{10,8},{12,10},{14,12},{16,14},{18,16},{20... | collective-permute-start | bytes 196616 | tf_op jit(solution)/shard_map/ppermute | solution.py:24
  42.5 5.9 %collective-permute-start.5 = (f32[1,4,1,32,128]{4,3,2,1,0:T(8,128)S(1)}, f32[1,4,1,32,128]{4,3,2,1,0:T(8,128)S(1)}, u32[]{:S(2)}, u32[]{:S(2)}) collective-permute-start(f32[1,4,1,32,128]{4,3,2,1,0:T(8,128)S(1)} %get-tuple-element.37), channel_id=1, source_target_pairs={{0,2},{2,4},{4,6},{6,8},{8,10},{10,12},{12,14},{14,16},{16,18},{18... | collective-permute-start | bytes 196616 | tf_op jit(solution)/shard_map/ppermute | solution.py:21
  48.5 5.5 %collective-permute-start.6 = (f32[1,4,34,1,128]{4,3,2,1,0:T(1,128)S(1)}, f32[1,4,34,1,128]{4,3,2,1,0:T(1,128)S(1)}, u32[]{:S(2)}, u32[]{:S(2)}) collective-permute-start(f32[1,4,34,1,128]{4,3,2,1,0:T(1,128)S(1)} %get-tuple-element.28), channel_id=1, source_target_pairs={{1,0},{3,2},{5,4},{7,6},{9,8},{11,10},{13,12},{15,14},{17,16},{19,... | collective-permute-start | bytes 208904 | tf_op jit(solution)/shard_map/ppermute | solution.py:24
  49.8 5.3 %collective-permute-start.7 = (f32[1,4,34,1,128]{4,3,2,1,0:T(1,128)S(1)}, f32[1,4,34,1,128]{4,3,2,1,0:T(1,128)S(1)}, u32[]{:S(2)}, u32[]{:S(2)}) collective-permute-start(f32[1,4,34,1,128]{4,3,2,1,0:T(1,128)S(1)} %get-tuple-element.29), channel_id=1, source_target_pairs={{0,1},{2,3},{4,5},{6,7},{8,9},{10,11},{12,13},{14,15},{16,17},{18,... | collective-permute-start | bytes 208904 | tf_op jit(solution)/shard_map/ppermute | solution.py:21
  76.3 5.6 %collective-permute-start.8 = (f32[1,4,1,32,128]{4,3,2,1,0:T(8,128)S(1)}, f32[1,4,1,32,128]{4,3,2,1,0:T(8,128)S(1)}, u32[]{:S(2)}, u32[]{:S(2)}) collective-permute-start(f32[1,4,1,32,128]{4,3,2,1,0:T(8,128)S(1)} %get-tuple-element.34), channel_id=1, source_target_pairs={{2,0},{4,2},{6,4},{8,6},{10,8},{12,10},{14,12},{16,14},{18,16},{20... | collective-permute-start | bytes 196616 | tf_op jit(solution)/shard_map/ppermute | solution.py:24
  77.6 5.6 %collective-permute-start.9 = (f32[1,4,1,32,128]{4,3,2,1,0:T(8,128)S(1)}, f32[1,4,1,32,128]{4,3,2,1,0:T(8,128)S(1)}, u32[]{:S(2)}, u32[]{:S(2)}) collective-permute-start(f32[1,4,1,32,128]{4,3,2,1,0:T(8,128)S(1)} %get-tuple-element.35), channel_id=1, source_target_pairs={{0,2},{2,4},{4,6},{6,8},{8,10},{10,12},{12,14},{14,16},{16,18},{18... | collective-permute-start | bytes 196616 | tf_op jit(solution)/shard_map/ppermute | solution.py:21
  83.3 5.3 %collective-permute-start.10 = (f32[1,4,34,1,128]{4,3,2,1,0:T(1,128)S(1)}, f32[1,4,34,1,128]{4,3,2,1,0:T(1,128)S(1)}, u32[]{:S(2)}, u32[]{:S(2)}) collective-permute-start(f32[1,4,34,1,128]{4,3,2,1,0:T(1,128)S(1)} %get-tuple-element.24), channel_id=1, source_target_pairs={{1,0},{3,2},{5,4},{7,6},{9,8},{11,10},{13,12},{15,14},{17,16},{19,... | collective-permute-start | bytes 208904 | tf_op jit(solution)/shard_map/ppermute | solution.py:24
  84.6 5.3 %collective-permute-start.11 = (f32[1,4,34,1,128]{4,3,2,1,0:T(1,128)S(1)}, f32[1,4,34,1,128]{4,3,2,1,0:T(1,128)S(1)}, u32[]{:S(2)}, u32[]{:S(2)}) collective-permute-start(f32[1,4,34,1,128]{4,3,2,1,0:T(1,128)S(1)} %get-tuple-element.25), channel_id=1, source_target_pairs={{0,1},{2,3},{4,5},{6,7},{8,9},{10,11},{12,13},{14,15},{16,17},{18,... | collective-permute-start | bytes 208904 | tf_op jit(solution)/shard_map/ppermute | solution.py:21
  111.1 17.5 %copy-start = (f32[1,2,2,32,32,128]{5,4,3,2,1,0:T(8,128)}, f32[1,2,2,32,32,128]{5,4,3,2,1,0:T(8,128)S(1)}, u32[]{:S(2)}) copy-start(f32[1,2,2,32,32,128]{5,4,3,2,1,0:T(8,128)S(1)} %copy.19) | copy-start | bytes 6291460
  111.1 5.9 %collective-permute-start.12 = (f32[1,4,1,32,128]{4,3,2,1,0:T(8,128)S(1)}, f32[1,4,1,32,128]{4,3,2,1,0:T(8,128)S(1)}, u32[]{:S(2)}, u32[]{:S(2)}) collective-permute-start(f32[1,4,1,32,128]{4,3,2,1,0:T(8,128)S(1)} %get-tuple-element.32), channel_id=1, source_target_pairs={{2,0},{4,2},{6,4},{8,6},{10,8},{12,10},{14,12},{16,14},{18,16},{20... | collective-permute-start | bytes 196616 | tf_op jit(solution)/shard_map/ppermute | solution.py:24
  112.4 5.9 %collective-permute-start.13 = (f32[1,4,1,32,128]{4,3,2,1,0:T(8,128)S(1)}, f32[1,4,1,32,128]{4,3,2,1,0:T(8,128)S(1)}, u32[]{:S(2)}, u32[]{:S(2)}) collective-permute-start(f32[1,4,1,32,128]{4,3,2,1,0:T(8,128)S(1)} %get-tuple-element.33), channel_id=1, source_target_pairs={{0,2},{2,4},{4,6},{6,8},{8,10},{10,12},{12,14},{14,16},{16,18},{18... | collective-permute-start | bytes 196616 | tf_op jit(solution)/shard_map/ppermute | solution.py:21
  118.4 5.9 %collective-permute-start.14 = (f32[1,4,34,1,128]{4,3,2,1,0:T(1,128)S(1)}, f32[1,4,34,1,128]{4,3,2,1,0:T(1,128)S(1)}, u32[]{:S(2)}, u32[]{:S(2)}) collective-permute-start(f32[1,4,34,1,128]{4,3,2,1,0:T(1,128)S(1)} %get-tuple-element.20), channel_id=1, source_target_pairs={{1,0},{3,2},{5,4},{7,6},{9,8},{11,10},{13,12},{15,14},{17,16},{19,... | collective-permute-start | bytes 208904 | tf_op jit(solution)/shard_map/ppermute | solution.py:24
  119.7 5.3 %collective-permute-start.15 = (f32[1,4,34,1,128]{4,3,2,1,0:T(1,128)S(1)}, f32[1,4,34,1,128]{4,3,2,1,0:T(1,128)S(1)}, u32[]{:S(2)}, u32[]{:S(2)}) collective-permute-start(f32[1,4,34,1,128]{4,3,2,1,0:T(1,128)S(1)} %get-tuple-element.21), channel_id=1, source_target_pairs={{0,1},{2,3},{4,5},{6,7},{8,9},{10,11},{12,13},{14,15},{16,17},{18,... | collective-permute-start | bytes 208904 | tf_op jit(solution)/shard_map/ppermute | solution.py:21
  148.5 2.3 %copy-start.1 = (f32[1,2,2,32,32,128]{5,4,3,2,1,0:T(8,128)S(1)}, f32[1,2,2,32,32,128]{5,4,3,2,1,0:T(8,128)}, u32[]{:S(2)}) copy-start(f32[1,2,2,32,32,128]{5,4,3,2,1,0:T(8,128)} %copy-done) | copy-start | bytes 6291460
  148.6 1.3 copy-start.12
Sparse Core Ops, SparseCore 0:
  152.2 46.0 all-gather.2
